TPU v7x, 32 devices: a whole 2x2x4 slice. The times are simulated.
32 devices in a mesh: row: 4 (over y, x), col: 8 (over z, core).
Axes of the slice: x: 2, y: 2, z: 4, core: 2. Of those that a mesh axis runs over, the one named last changes fastest.
Arguments:
- tokens: bfloat16 [1024, 53248], P(('row', 'col')), may hold values from -6 to 6
- eigvecs: float32 [53248, 2048], P('row', 'col'), may hold values from -0.02734375 to 0.02734375
- eigvals: float32 [2048], P('col'), may hold values from 0.25 to 4
- v_first: float32 [53248, 256], P(('row', 'col')), may hold values from -0.109375 to 0.109375
- v_second: float32 [53248, 256], P(('row', 'col')), may hold values from -0.109375 to 0.109375
- t_first: float32 [256, 256], replicated, may hold values from -0.375 to 0.375
- t_second: float32 [256, 256], replicated, may hold values from -0.375 to 0.375
Outputs:
- whitened: float32 [1024, 2048], P('row', 'col')
All inputs are finite; a program needn't handle non-finite values.
Results may differ from a plain program's by a relative error of at most 0.0029.
Values may be sent and summed in bfloat16 or wider, within the bound.
No kernel may reach another device: no remote copies, remote signals or barrier semaphores. Data moves between devices by JAX's collectives and lax.ppermute only.
A program may use at most 128 MiB of HBM per device.

v0:
```python
import jax
import jax.numpy as jnp
from jax import lax
from jax.sharding import PartitionSpec as P


def local_update(block, panel, factor, inner):
    middle = jnp.dot(
        factor, inner, precision=lax.Precision.HIGHEST, preferred_element_type=jnp.float32
    )
    return block - jnp.dot(
        panel, middle, precision=lax.Precision.HIGHEST, preferred_element_type=jnp.float32
    )


def partial_inner(panel, block):
    return jnp.dot(
        panel.T, block, precision=lax.Precision.HIGHEST, preferred_element_type=jnp.float32
    )


def per_device(tokens, eigvecs, eigvals, v_first, v_second, t_first, t_second):
    block = lax.all_to_all(eigvecs, "col", split_axis=0, concat_axis=1, tiled=True)
    for panel, factor in ((v_second, t_second), (v_first, t_first)):
        inner = lax.psum(partial_inner(panel, block), ("row", "col"))
        block = local_update(block, panel, factor, inner)
    every_value = lax.all_gather(eigvals, "col", axis=0, tiled=True)
    whitening = (block * lax.rsqrt(every_value)[None, :]).astype(jnp.bfloat16)
    slab = lax.all_to_all(tokens, ("row", "col"), split_axis=1, concat_axis=0, tiled=True)
    partial_value = jnp.dot(slab, whitening, preferred_element_type=jnp.float32)
    by_column = lax.psum_scatter(partial_value, "col", scatter_dimension=1, tiled=True)
    summed = lax.psum_scatter(by_column, "row", scatter_dimension=0, tiled=True)
    return summed


def solution(mesh):
    in_specs = (
        P(("row", "col"), None),
        P("row", "col"),
        P("col"),
        P(("row", "col"), None),
        P(("row", "col"), None),
        P(),
        P(),
    )
    out_specs = P("row", "col")
    return jax.shard_map(
        per_device, mesh=mesh, in_specs=in_specs, out_specs=out_specs, check_vma=False
    )
```

profile of v0, /device:TPU:0, one launch (start us, length us, event | category | flops | bytes accessed | tf_op | source)
XLA Modules:
  0.0 837.7 jit_solution(9575933095389601247)
XLA Ops:
  6.5 13.8 %copy.15 = f32[8,1664,256]{1,2,0:T(8,128)} copy(f32[8,1664,256]{2,1,0:T(8,128)} %bitcast.39) | data formatting | bytes 27262976 | tf_op jit(solution)/shard_map/all_to_all | solution.py:23
  20.4 6.4 all-to-all-start
  26.7 4.1 copy.20
  30.8 292.2 %all-to-all-done = f32[8,1664,256]{1,2,0:T(8,128)} async-done(((f32[8,1664,256]{1,2,0:T(8,128)}), f32[8,1664,256]{1,2,0:T(8,128)}, u32[]{:S(2)}, u32[]{:S(2)}) %all-to-all-start) | async-done | bytes 13631520 | tf_op jit(solution)/shard_map/all_to_all | solution.py:23
  323.0 4.1 all-to-all-start.1
  327.2 0.0 all-reduce.3.cloned.1.call-start
  327.2 25.8 %fusion.2 = f32[256,2048]{1,0:T(8,128)} fusion(f32[1664,256]{1,0:T(8,128)S(1)} %copy-done, f32[1664,2048]{0,1:T(8,128)} %bitcast.2), kind=kOutput, calls=%fused_computation.7 | convolution fusion | flops 10468982784 | bytes 17432576 | tf_op jit(solution)/shard_map/dot_general | solution.py:17
  353.1 0.0 all-reduce.3.cloned.1.call-update
  353.1 0.2 all-reduce.5.cloned.1.call-start
  353.3 151.8 %all-reduce.3.cloned.1.call-done = f32[256,2048]{1,0:T(8,128)} async-done(((f32[256,2048]{1,0:T(8,128)}), f32[256,2048]{1,0:T(8,128)}) %all-reduce.3.cloned.1.call-update) | async-done | bytes 2097168 | tf_op jit(solution)/shard_map/psum | solution.py:25
  505.2 5.2 fusion.3
  510.3 0.0 copy-start.3
  510.3 16.9 %bitcast_subtract_fusion.1 = f32[1664,2048]{0,1:T(8,128)S(1)} fusion(f32[1664,2048]{0,1:T(8,128)} %bitcast.2, f32[2048,256]{1,0:T(8,128)S(1)} %fusion.3, f32[1664,256]{1,0:T(8,128)S(1)} %copy-done), kind=kOutput, calls=%fused_computation.3 | convolution fusion | flops 10472390656 | bytes 31064064 | tf_op jit(solution)/shard_map/dot_general | solution.py:11
  527.3 4.9 copy-done.2
  532.1 13.1 %convolution_bitcast_fusion.1 = f32[256,2048]{0,1:T(8,128)} fusion(f32[1664,2048]{0,1:T(8,128)S(1)} %bitcast_subtract_fusion.1, f32[1664,256]{1,0:T(8,128)S(1)} %copy-done.3), kind=kOutput, calls=%fused_computation.6 | convolution fusion | flops 10468982784 | bytes 17432576 | tf_op jit(solution)/shard_map/dot_general | solution.py:17
  545.3 0.0 all-reduce.5.cloned.1.call-update
  545.3 0.0 reduce-scatter.3.cloned.1.call-start
  545.4 0.6 copy-done.6
  546.0 10.6 %all-gather = f32[8,1,256]{2,1,0:T(1,128)S(1)} all-gather(f32[1,1,256]{2,1,0:T(1,128)S(1)} %bitcast.43), channel_id=1, replica_groups=mesh['row'=4,'col'=8] {'col'}, dimensions={0}, use_global_device_ids=true | all-gather | bytes 9216 | tf_op jit(solution)/shard_map/all_gather | solution.py:27
  556.6 122.3 %all-reduce.5.cloned.1.call-done = f32[256,2048]{0,1:T(8,128)} async-done(((f32[256,2048]{0,1:T(8,128)}), f32[256,2048]{0,1:T(8,128)}) %all-reduce.5.cloned.1.call-update) | async-done | bytes 2097168 | tf_op jit(solution)/shard_map/psum | solution.py:25
  678.9 3.5 fusion.4
  682.4 16.4 %fusion.1 = bf16[1664,2048]{0,1:T(8,128)(2,1)} fusion(f32[1664,2048]{0,1:T(8,128)} %copy-done.2, f32[2048,256]{1,0:T(8,128)S(1)} %fusion.4, f32[1664,256]{1,0:T(8,128)S(1)} %copy-done.3, f32[2048]{0:T(1024)S(1)} %bitcast.42), kind=kOutput, calls=%fused_computation.2 | convolution fusion | flops 10479206400 | bytes 24256512 | tf_op jit(solution)/shard_map/dot_general | solution.py:11
  698.8 0.0 all-to-all-done.1
  698.8 12.9 %convolution_bitcast_fusion = f32[1024,2048]{0,1:T(8,128)} fusion(bf16[1664,2048]{0,1:T(8,128)(2,1)} %fusion.1, bf16[1024,1664]{1,0:T(8,128)(2,1)} %bitcast.10), kind=kOutput, calls=%fused_computation.4 | convolution fusion | flops 6979321856 | bytes 18612224 | tf_op jit(solution)/shard_map/dot_general | solution.py:30
  711.8 0.0 reduce-scatter.3.cloned.1.call-update
  711.8 0.0 copy-start.1
  711.8 0.0 reduce-scatter.5.cloned.1.call-start
  711.9 88.4 %reduce-scatter.3.cloned.1.call-done = f32[1024,256]{0,1:T(8,128)} async-done(((f32[1024,2048]{0,1:T(8,128)}), f32[1024,256]{0,1:T(8,128)}) %reduce-scatter.3.cloned.1.call-update) | async-done | bytes 1048592 | tf_op jit(solution)/shard_map/reduce_scatter | solution.py:31
  800.2 0.0 reduce-scatter.5.cloned.1.call-update
  800.2 29.2 %reduce-scatter.5.cloned.1.call-done = f32[256,256]{0,1:T(8,128)} async-done(((f32[1024,256]{0,1:T(8,128)}), f32[256,256]{0,1:T(8,128)}) %reduce-scatter.5.cloned.1.call-update) | async-done | bytes 262160 | tf_op jit(solution)/shard_map/reduce_scatter | solution.py:32
  829.4 1.8 copy.17
  831.2 0.0 copy-done.1
  (10 shorter events, 0.0 us)
Async XLA Ops:
  6.5 320.7 %copy-start = (f32[1664,256]{1,0:T(8,128)S(1)}, f32[1664,256]{1,0:T(8,128)}, u32[]{:S(2)}) copy-start(f32[1664,256]{1,0:T(8,128)} %param.11) | copy-start | bytes 5111812
  20.4 302.7 %all-to-all-start = ((f32[8,1664,256]{1,2,0:T(8,128)}), f32[8,1664,256]{1,2,0:T(8,128)}, u32[]{:S(2)}, u32[]{:S(2)}) async-start(f32[8,1664,256]{1,2,0:T(8,128)} %copy.15), calls=%async_computation | async-start | bytes 27262976 | tf_op jit(solution)/shard_map/all_to_all | solution.py:23
  323.0 375.8 %all-to-all-start.1 = ((bf16[32,32,1664]{2,0,1:T(8,128)(2,1)}), bf16[32,32,1664]{2,0,1:T(8,128)(2,1)}, u32[]{:S(2)}, u32[]{:S(2)}) async-start(bf16[32,32,1664]{2,0,1:T(8,128)(2,1)} %bitcast.40), calls=%async_computation.1 | async-start | bytes 6815744 | tf_op jit(solution)/shard_map/all_to_all | solution.py:29
  327.2 178.0 %all-reduce.3.cloned.1.call-start = ((), (), s32[]{:S(2)}) async-start(), calls=%async_computation.4 | async-start | bytes 4194304 | tf_op jit(solution)/shard_map/psum | solution.py:25
  353.1 152.1 %copy-start.4 = (f32[256,256]{1,0:T(8,128)S(1)}, f32[256,256]{1,0:T(8,128)}, u32[]{:S(2)}) copy-start(f32[256,256]{1,0:T(8,128)} %param.13) | copy-start | bytes 786436
  353.1 325.8 %all-reduce.5.cloned.1.call-start = ((), (), s32[]{:S(2)}) async-start(), calls=%async_computation.5 | async-start | bytes 4194304 | tf_op jit(solution)/shard_map/psum | solution.py:25
  510.3 21.8 %copy-start.3 = (f32[1664,256]{1,0:T(8,128)S(1)}, f32[1664,256]{1,0:T(8,128)}, u32[]{:S(2)}) copy-start(f32[1664,256]{1,0:T(8,128)} %param.10) | copy-start | bytes 5111812
  527.2 4.9 copy-start.2
  545.3 0.7 copy-start.6
  545.3 133.6 %copy-start.5 = (f32[256,256]{1,0:T(8,128)S(1)}, f32[256,256]{1,0:T(8,128)}, u32[]{:S(2)}) copy-start(f32[256,256]{1,0:T(8,128)} %param.12) | copy-start | bytes 786436
  545.3 254.9 %reduce-scatter.3.cloned.1.call-start = ((), (), s32[]{:S(2)}) async-start(), calls=%async_computation.6 | async-start | bytes 9437184 | tf_op jit(solution)/shard_map/reduce_scatter | solution.py:31
  711.8 119.4 %copy-start.1 = (f32[1664,256]{1,0:T(8,128)S(1)}, f32[1664,256]{1,0:T(8,128)}, u32[]{:S(2)}) copy-start(f32[1664,256]{1,0:T(8,128)} %param.11) | copy-start | bytes 5111812
  711.8 117.6 %reduce-scatter.5.cloned.1.call-start = ((), (), s32[]{:S(2)}) async-start(), calls=%async_computation.7 | async-start | bytes 1310720 | tf_op jit(solution)/shard_map/reduce_scatter | solution.py:32
Sparse Core Ops, SparseCore 0:
  353.2 151.8 all-reduce.2
  545.4 133.4 all-reduce.4
  711.9 88.2 reduce-scatter.2
  803.0 26.4 reduce-scatter.4
where the time goes:
time: 838 us
  waiting for transfers between devices  684 us (82%)
  matrix products  93.9 us (11%)
  local copies, waits for them, and re-layouts  25.3 us (3%)
  between operations  13.2 us (2%)
  starting transfers between devices  10.8 us (1%)
  blocking collectives  10.6 us (1%)
    all_to_all x1, waiting for transfers between devices, per_device(): lax.all_to_all(eigvecs, 'col', split_axis=0, concat_axis=1, tiled=True)  292 us
    psum x2, waiting for transfers between devices, per_device(): inner = lax.psum(partial_inner(panel, block), ('row', 'col'))  274 us
    reduce_scatter x1, waiting for transfers between devices, per_device(): lax.psum_scatter(partial_value, 'col', scatter_dimension=1, tiled=True)  88.4 us
    dot_general x2, matrix products, partial_inner(): jnp.dot(panel.T, block, precision=lax.Precision.HIGHEST, preferred_elemen...  39 us
    dot_general x2, matrix products, local_update(): jnp.dot(panel, middle, precision=lax.Precision.HIGHEST, preferred_element...  33.3 us
    reduce_scatter x1, waiting for transfers between devices, per_device(): summed = lax.psum_scatter(by_column, 'row', scatter_dimension=0, tiled=True)  29.2 us
  transfers between devices with their start and end apart: 6, of which 5 were waited for; matrix products, arithmetic and copies ran while one was open for 10% of the time, Pallas kernels for 0%

commit v1 on v0

--- a/solution.py
+++ b/solution.py
@@ -22,7 +22,7 @@
 def per_device(tokens, eigvecs, eigvals, v_first, v_second, t_first, t_second):
     block = lax.all_to_all(eigvecs, "col", split_axis=0, concat_axis=1, tiled=True)
     for panel, factor in ((v_second, t_second), (v_first, t_first)):
-        inner = lax.psum(partial_inner(panel, block), ("row", "col"))
+        inner = lax.psum(lax.psum(partial_inner(panel, block), "col"), "row")
         block = local_update(block, panel, factor, inner)
     every_value = lax.all_gather(eigvals, "col", axis=0, tiled=True)
     whitening = (block * lax.rsqrt(every_value)[None, :]).astype(jnp.bfloat16)

time: 838 us -> 870 us (1.038); the launches traced: 838 us -> 860 us
  blocking collectives: 10.6 us -> 313 us
  waiting for transfers between devices: 684 us -> 407 us
    all_to_all x0 -> x1, blocking collectives: none -> 303 us  [per_device(): lax.all_to_all(eigvecs, 'col', split_axis=0, concat_axis=1, tiled=True)]
    all_to_all x1 -> x0, waiting for transfers between devices: 292 us -> none  [per_device(): lax.all_to_all(eigvecs, 'col', split_axis=0, concat_axis=1, tiled=True)]
    psum x2 -> x4, waiting for transfers between devices: 274 us -> 288 us  [per_device(): inner = lax.psum(lax.psum(partial_inner(panel, block), 'col'), 'row')]
  transfers between devices with their start and end apart: 6 -> 7, of which waited for: 5 -> 6; matrix products, arithmetic and copies ran while one was open for 10% -> 7% of each run, Pallas kernels for 0% -> 0%
where the time goes in v1:
time: 870 us; the launch traced here: 860 us
  waiting for transfers between devices  407 us (47%)
  blocking collectives  313 us (36%)
  matrix products  91.7 us (11%)
  local copies, waits for them, and re-layouts  29.5 us (3%)
  between operations  14 us (2%)
    all_to_all x1, blocking collectives, per_device(): lax.all_to_all(eigvecs, 'col', split_axis=0, concat_axis=1, tiled=True)  303 us
    psum x4, waiting for transfers between devices, per_device(): inner = lax.psum(lax.psum(partial_inner(panel, block), 'col'), 'row')  288 us
    reduce_scatter x1, waiting for transfers between devices, per_device(): lax.psum_scatter(partial_value, 'col', scatter_dimension=1, tiled=True)  89.6 us
    dot_general x2, matrix products, partial_inner(): jnp.dot(panel.T, block, precision=lax.Precision.HIGHEST, preferred_elemen...  36.5 us
    dot_general x2, matrix products, local_update(): jnp.dot(panel, middle, precision=lax.Precision.HIGHEST, preferred_element...  33.5 us
    reduce_scatter x1, waiting for transfers between devices, per_device(): summed = lax.psum_scatter(by_column, 'row', scatter_dimension=0, tiled=True)  29.2 us
  transfers between devices with their start and end apart: 7, of which 6 were waited for; matrix products, arithmetic and copies ran while one was open for 7% of the time, Pallas kernels for 0%

profile of v1, /device:TPU:0, one launch (start us, length us, event | category | flops | bytes accessed | tf_op | source)
XLA Modules:
  0.0 860.2 jit_solution(3578963951012251666)
XLA Ops:
  6.5 13.9 %copy.15 = f32[8,1664,256]{1,2,0:T(8,128)} copy(f32[8,1664,256]{2,1,0:T(8,128)} %bitcast.41) | data formatting | bytes 27262976 | tf_op jit(solution)/shard_map/all_to_all | solution.py:23
  20.4 302.6 %all_to_all.38 = f32[8,1664,256]{1,2,0:T(8,128)S(1)} all-to-all(f32[8,1664,256]{1,2,0:T(8,128)} %copy.15), channel_id=1, replica_groups=mesh['row'=4,'col'=8] {'col'}, dimensions={0} | all-to-all | bytes 27262976 | tf_op jit(solution)/shard_map/all_to_all | solution.py:23
  323.0 4.9 copy-done.3
  327.9 23.4 %fusion.2 = f32[256,2048]{1,0:T(8,128)} fusion(f32[1664,256]{1,0:T(8,128)S(1)} %copy-done, f32[1664,2048]{0,1:T(8,128)S(1)} %bitcast.39), kind=kOutput, calls=%fused_computation.7 | convolution fusion | flops 10468982784 | bytes 17432576 | tf_op jit(solution)/shard_map/dot_general | solution.py:17
  351.3 0.0 all-reduce.5.cloned.1.call-update
  351.3 0.0 all-reduce.7.cloned.1.call-start
  351.4 64.2 %all-reduce.5.cloned.1.call-done = f32[256,2048]{1,0:T(8,128)} async-done(((f32[256,2048]{1,0:T(8,128)}), f32[256,2048]{1,0:T(8,128)}) %all-reduce.5.cloned.1.call-update) | async-done | bytes 2097168 | tf_op jit(solution)/shard_map/psum | solution.py:25
  415.5 0.0 all-reduce.7.cloned.1.call-update
  415.6 4.0 copy.20
  419.6 4.3 all-to-all-start.1
  423.9 0.0 all-reduce.9.cloned.1.call-start
  424.0 97.7 %all-reduce.7.cloned.1.call-done = f32[256,2048]{1,0:T(8,128)} async-done(((f32[256,2048]{1,0:T(8,128)}), f32[256,2048]{1,0:T(8,128)}) %all-reduce.7.cloned.1.call-update) | async-done | bytes 2097168 | tf_op jit(solution)/shard_map/psum | solution.py:25
  521.7 5.2 fusion.3
  526.9 17.1 %bitcast_subtract_fusion.1 = f32[1664,2048]{0,1:T(8,128)S(1)} fusion(f32[1664,2048]{0,1:T(8,128)} %bitcast.40, f32[2048,256]{1,0:T(8,128)S(1)} %fusion.3, f32[1664,256]{1,0:T(8,128)S(1)} %copy-done), kind=kOutput, calls=%fused_computation.3 | convolution fusion | flops 10472390656 | bytes 31064064 | tf_op jit(solution)/shard_map/dot_general | solution.py:11
  544.0 4.9 copy-done.2
  548.8 13.1 %convolution_bitcast_fusion.1 = f32[256,2048]{0,1:T(8,128)} fusion(f32[1664,2048]{0,1:T(8,128)S(1)} %bitcast_subtract_fusion.1, f32[1664,256]{1,0:T(8,128)S(1)} %copy-done.4), kind=kOutput, calls=%fused_computation.6 | convolution fusion | flops 10468982784 | bytes 17432576 | tf_op jit(solution)/shard_map/dot_general | solution.py:17
  562.0 0.0 all-reduce.9.cloned.1.call-update
  562.0 0.0 all-reduce.11.cloned.1.call-start
  562.0 65.2 %all-reduce.9.cloned.1.call-done = f32[256,2048]{0,1:T(8,128)} async-done(((f32[256,2048]{0,1:T(8,128)}), f32[256,2048]{0,1:T(8,128)}) %all-reduce.9.cloned.1.call-update) | async-done | bytes 2097168 | tf_op jit(solution)/shard_map/psum | solution.py:25
  627.2 0.0 all-reduce.11.cloned.1.call-update
  627.3 0.0 reduce-scatter.3.cloned.1.call-start
  627.3 10.7 %all-gather = f32[8,1,256]{2,1,0:T(1,128)S(1)} all-gather(f32[1,1,256]{2,1,0:T(1,128)S(1)} %bitcast.45), channel_id=1, replica_groups=mesh['row'=4,'col'=8] {'col'}, dimensions={0}, use_global_device_ids=true | all-gather | bytes 9216 | tf_op jit(solution)/shard_map/all_gather | solution.py:27
  638.0 61.3 %all-reduce.11.cloned.1.call-done = f32[256,2048]{0,1:T(8,128)} async-done(((f32[256,2048]{0,1:T(8,128)}), f32[256,2048]{0,1:T(8,128)}) %all-reduce.11.cloned.1.call-update) | async-done | bytes 2097168 | tf_op jit(solution)/shard_map/psum | solution.py:25
  699.3 3.5 fusion.4
  702.8 16.4 %fusion.1 = bf16[1664,2048]{0,1:T(8,128)(2,1)} fusion(f32[1664,2048]{0,1:T(8,128)} %copy-done.2, f32[2048,256]{1,0:T(8,128)S(1)} %fusion.4, f32[1664,256]{1,0:T(8,128)S(1)} %copy-done.4, f32[2048]{0:T(1024)S(1)} %bitcast.44), kind=kOutput, calls=%fused_computation.2 | convolution fusion | flops 10479206400 | bytes 24256512 | tf_op jit(solution)/shard_map/dot_general | solution.py:11
  719.3 12.9 %convolution_bitcast_fusion = f32[1024,2048]{0,1:T(8,128)} fusion(bf16[1664,2048]{0,1:T(8,128)(2,1)} %fusion.1, bf16[1024,1664]{1,0:T(8,128)(2,1)} %bitcast.10), kind=kOutput, calls=%fused_computation.4 | convolution fusion | flops 6979321856 | bytes 18612224 | tf_op jit(solution)/shard_map/dot_general | solution.py:30
  732.2 0.0 reduce-scatter.3.cloned.1.call-update
  732.3 0.0 reduce-scatter.5.cloned.1.call-start
  732.3 89.6 %reduce-scatter.3.cloned.1.call-done = f32[1024,256]{0,1:T(8,128)} async-done(((f32[1024,2048]{0,1:T(8,128)}), f32[1024,256]{0,1:T(8,128)}) %reduce-scatter.3.cloned.1.call-update) | async-done | bytes 1048592 | tf_op jit(solution)/shard_map/reduce_scatter | solution.py:31
  821.9 0.0 reduce-scatter.5.cloned.1.call-update
  822.0 29.2 %reduce-scatter.5.cloned.1.call-done = f32[256,256]{0,1:T(8,128)} async-done(((f32[1024,256]{0,1:T(8,128)}), f32[256,256]{0,1:T(8,128)}) %reduce-scatter.5.cloned.1.call-update) | async-done | bytes 262160 | tf_op jit(solution)/shard_map/reduce_scatter | solution.py:32
  851.1 1.8 copy.17
  (17 shorter events, 0.1 us)
Async XLA Ops:
  6.5 321.3 %copy-start = (f32[1664,256]{1,0:T(8,128)S(1)}, f32[1664,256]{1,0:T(8,128)}, u32[]{:S(2)}) copy-start(f32[1664,256]{1,0:T(8,128)} %param.11) | copy-start | bytes 5111812
  6.5 409.0 %all-reduce.5.cloned.1.call-start = ((), (), s32[]{:S(2)}) async-start(), calls=%async_computation.4 | async-start | bytes 4194304 | tf_op jit(solution)/shard_map/psum | solution.py:25
  323.0 4.9 copy-start.3
  351.3 170.4 %all-reduce.7.cloned.1.call-start = ((), (), s32[]{:S(2)}) async-start(), calls=%async_computation.5 | async-start | bytes 4194304 | tf_op jit(solution)/shard_map/psum | solution.py:25
  419.6 102.1 %copy-start.5 = (f32[256,256]{1,0:T(8,128)S(1)}, f32[256,256]{1,0:T(8,128)}, u32[]{:S(2)}) copy-start(f32[256,256]{1,0:T(8,128)} %param.13) | copy-start | bytes 786436
  419.6 299.7 %all-to-all-start.1 = ((bf16[32,32,1664]{2,0,1:T(8,128)(2,1)}), bf16[32,32,1664]{2,0,1:T(8,128)(2,1)}, u32[]{:S(2)}, u32[]{:S(2)}) async-start(bf16[32,32,1664]{2,0,1:T(8,128)(2,1)} %bitcast.42), calls=%async_computation.1 | async-start | bytes 6815744 | tf_op jit(solution)/shard_map/all_to_all | solution.py:29
  423.9 203.3 %all-reduce.9.cloned.1.call-start = ((), (), s32[]{:S(2)}) async-start(), calls=%async_computation.6 | async-start | bytes 4194304 | tf_op jit(solution)/shard_map/psum | solution.py:25
  526.8 22.0 %copy-start.4 = (f32[1664,256]{1,0:T(8,128)S(1)}, f32[1664,256]{1,0:T(8,128)}, u32[]{:S(2)}) copy-start(f32[1664,256]{1,0:T(8,128)} %param.10) | copy-start | bytes 5111812
  544.0 4.9 copy-start.2
  562.0 65.3 %copy-start.7 = (f32[256]{0:T(256)S(1)}, f32[256]{0:T(256)}, u32[]{:S(2)}) copy-start(f32[256]{0:T(256)} %param.9) | copy-start | bytes 3076
  562.0 137.3 %copy-start.6 = (f32[256,256]{1,0:T(8,128)S(1)}, f32[256,256]{1,0:T(8,128)}, u32[]{:S(2)}) copy-start(f32[256,256]{1,0:T(8,128)} %param.12) | copy-start | bytes 786436
  562.0 137.3 %all-reduce.11.cloned.1.call-start = ((), (), s32[]{:S(2)}) async-start(), calls=%async_computation.7 | async-start | bytes 4194304 | tf_op jit(solution)/shard_map/psum | solution.py:25
  627.3 194.7 %reduce-scatter.3.cloned.1.call-start = ((), (), s32[]{:S(2)}) async-start(), calls=%async_computation.8 | async-start | bytes 9437184 | tf_op jit(solution)/shard_map/reduce_scatter | solution.py:31
  732.2 120.7 %copy-start.1 = (f32[1664,256]{1,0:T(8,128)S(1)}, f32[1664,256]{1,0:T(8,128)}, u32[]{:S(2)}) copy-start(f32[1664,256]{1,0:T(8,128)} %param.11) | copy-start | bytes 5111812
  732.3 118.9 %reduce-scatter.5.cloned.1.call-start = ((), (), s32[]{:S(2)}) async-start(), calls=%async_computation.9 | async-start | bytes 1310720 | tf_op jit(solution)/shard_map/reduce_scatter | solution.py:32
Sparse Core Ops, SparseCore 0:
  351.4 64.0 all-reduce.4
  418.6 102.9 all-reduce.6
  562.1 65.0 all-reduce.8
  630.2 69.0 all-reduce.10
  732.4 89.5 reduce-scatter.2
  824.7 26.4 reduce-scatter.4
